TPU v7x, 512 devices: a whole 4x8x8 slice. The times are simulated.
512 devices in a mesh: dp: 64 (over y, z), fsdp: 8 (over x, core).
Axes of the slice: x: 4, y: 8, z: 8, core: 2. Of those that a mesh axis runs over, the one named last changes fastest.
Arguments:
- frames: bfloat16 [524288, 512], P(('dp', 'fsdp')), may hold values from -6 to 6
- utt_pairs: int32 [8, 64, 4], P('fsdp'), may hold values from 32 to 256, as said below
- utt_dest: int32 [8, 64, 4], P('fsdp'), may hold values from 0 to 63, as said below
- conv_weight: bfloat16 [1536, 512], P('dp'), may hold values from -0.15625 to 0.15625
- proj_weight: bfloat16 [512, 1536], P('dp'), may hold values from -0.25 to 0.25
- point_weight: bfloat16 [2, 1536, 1536], P(None, None, 'fsdp'), may hold values from -0.15625 to 0.15625
- depth_weight: float32 [31, 1536], replicated, may hold values from -1 to 1
- gain_first: float32 [1536], replicated, may hold values from 0.5 to 1.5
- gain_second: float32 [1536], replicated, may hold values from 0.5 to 1.5
Outputs:
- encoded: bfloat16 [262144, 1536], P(('dp', 'fsdp'))
Inputs may be any that keep to these rules, and one draw needn't show every extreme that they name: `utt_pairs`: every loader holds exactly 512 pairs and every sequence device receives exactly 512 pairs, from 4 different loaders. Each loader holds one utterance of exactly 256 pairs and one of exactly 32 pairs. `utt_dest`: the 4 utterances of loader i go to the 4 different sequence devices (i + k * 64 / 4) mod 64, k = 0 .. 3, in some order.
All inputs are finite; a program needn't handle non-finite values.
Results may differ from a plain program's by a relative error of at most 0.012.
Values may be sent and summed in bfloat16 or wider, within the bound.
No kernel may reach another device: no remote copies, remote signals or barrier semaphores. Data moves between devices by JAX's collectives and lax.ppermute only.
A program may use at most 64 MiB of HBM per device.

v0:
```python
import jax
import jax.numpy as jnp
from jax import lax
from jax.sharding import PartitionSpec as P


def passed_along(value, axis, steps):
    count = lax.axis_size(axis)
    pairs = [(source, (source + steps) % count) for source in range(count)]
    return lax.ppermute(value, axis, pairs)


def frontend(pair_rows, first_rows, conv_full):
    channels = pair_rows.shape[1] // 2
    even_frames = pair_rows[:, :channels]
    odd_frames = pair_rows[:, channels:]
    earlier = jnp.pad(odd_frames[:-1], ((1, 0), (0, 0)))
    earlier = jnp.where(first_rows[:, None], jnp.zeros_like(earlier), earlier)
    summed = jnp.dot(earlier, conv_full[:channels], preferred_element_type=jnp.float32)
    summed = summed + jnp.dot(
        even_frames, conv_full[channels : 2 * channels], preferred_element_type=jnp.float32
    )
    summed = summed + jnp.dot(
        odd_frames, conv_full[2 * channels :], preferred_element_type=jnp.float32
    )
    return jax.nn.relu(summed).astype(jnp.bfloat16)


def layer_norm(values, scales):
    centered = values - jnp.mean(values, axis=-1, keepdims=True)
    variance = jnp.mean(centered * centered, axis=-1, keepdims=True)
    return centered * lax.rsqrt(variance + 1e-05) * scales


def depthwise(gated, depth_weight, positions, lengths):
    row_count = gated.shape[0]
    kernel_size = depth_weight.shape[0]
    half_width = kernel_size // 2
    padded = jnp.pad(gated.astype(jnp.float32), ((half_width, half_width), (0, 0)))
    mixed = jnp.zeros(gated.shape, jnp.float32)
    for tap_index in range(kernel_size):
        offset = tap_index - half_width
        inside = (positions + offset >= 0) & (positions + offset < lengths)
        term = padded[tap_index : tap_index + row_count] * depth_weight[tap_index][None, :]
        mixed = mixed + jnp.where(inside[:, None], term, jnp.zeros_like(term))
    return mixed


def gate_product(normed, value_weight, gate_weight):
    value_part = jnp.dot(normed, value_weight, preferred_element_type=jnp.float32)
    gate_part = jnp.dot(normed, gate_weight, preferred_element_type=jnp.float32)
    return (value_part * jax.nn.sigmoid(gate_part)).astype(jnp.bfloat16)


def cut_pieces(source_rows, own_starts, slot_size, utt_count):
    padded = jnp.pad(source_rows, ((0, slot_size), (0, 0)))
    pieces = []
    for slot_index in range(utt_count):
        pieces.append(lax.dynamic_slice_in_dim(padded, own_starts[slot_index], slot_size, 0))
    return pieces


def body(
    frames,
    utt_pairs,
    utt_dest,
    conv_weight,
    proj_weight,
    point_weight,
    depth_weight,
    gain_first,
    gain_second,
):
    node_count = lax.axis_size("dp")
    own_index = lax.axis_index("dp")
    pair_count = frames.shape[0] // 2
    channels = frames.shape[1]
    utt_count = utt_pairs.shape[2]
    spacing = node_count // utt_count
    slot_size = pair_count // 2
    pair_table = utt_pairs[0]
    dest_table = utt_dest[0]
    loader_ids = jnp.arange(node_count, dtype=jnp.int32)
    slot_ids = jnp.arange(utt_count, dtype=jnp.int32)
    slot_table = (dest_table - loader_ids[:, None]) % node_count // spacing
    matches = (slot_table[:, :, None] == slot_ids[None, None, :]).astype(jnp.int32)
    loader_offsets = jnp.cumsum(pair_table, axis=1) - pair_table
    slot_counts = jnp.sum(matches * pair_table[:, :, None], axis=1)
    slot_starts = jnp.sum(matches * loader_offsets[:, :, None], axis=1)
    conv_full, proj_full = (
        lax.all_gather(conv_weight, "dp", axis=0, tiled=True),
        lax.all_gather(proj_weight, "dp", axis=0, tiled=True),
    )
    own_starts = slot_starts[own_index]
    sources = (own_index - slot_ids * spacing) % node_count
    piece_lengths = slot_counts[sources, slot_ids]
    earlier_pieces = (sources[None, :] < sources[:, None]).astype(jnp.int32)
    piece_offsets = jnp.sum(earlier_pieces * piece_lengths[None, :], axis=1)
    pair_rows = jnp.arange(pair_count, dtype=jnp.int32)
    inside = (
        (pair_rows[:, None] >= piece_offsets[None, :])
        & (pair_rows[:, None] < piece_offsets[None, :] + piece_lengths[None, :])
    ).astype(jnp.int32)
    piece_index = jnp.sum(inside * slot_ids[None, :], axis=1)
    positions = pair_rows - jnp.sum(inside * piece_offsets[None, :], axis=1)
    lengths = jnp.sum(inside * piece_lengths[None, :], axis=1)
    flat_slot = piece_index * slot_size + positions
    frame_pairs = frames.reshape(pair_count, 2 * channels)
    pieces = cut_pieces(frame_pairs, own_starts, slot_size, utt_count)
    arrived = [pieces[0]]
    for slot_index in range(1, utt_count):
        arrived.append(passed_along(pieces[slot_index], "dp", slot_index * spacing))
    stacked = jnp.concatenate(arrived, axis=0)
    packed = jnp.take(stacked, flat_slot, axis=0)
    front = frontend(packed, positions == 0, conv_full)
    projected = jnp.dot(front, proj_full, preferred_element_type=jnp.float32).astype(jnp.bfloat16)
    normed = layer_norm(projected.astype(jnp.float32), gain_first).astype(jnp.bfloat16)
    weight_part = lax.all_gather(point_weight, "fsdp", axis=2, tiled=True)
    gated = gate_product(normed, weight_part[0], weight_part[1])
    mixed = depthwise(gated, depth_weight, positions, lengths)
    scaled = layer_norm(mixed, gain_second)
    return (scaled * jax.nn.sigmoid(scaled)).astype(jnp.bfloat16)


def solution(mesh):
    in_specs = (
        P(("dp", "fsdp"), None),
        P("fsdp", None, None),
        P("fsdp", None, None),
        P("dp", None),
        P("dp", None),
        P(None, None, "fsdp"),
        P(),
        P(),
        P(),
    )
    out_specs = P(("dp", "fsdp"), None)
    return jax.shard_map(body, mesh=mesh, in_specs=in_specs, out_specs=out_specs, check_vma=False)
```

profile of v0, /device:TPU:1, one launch (start us, length us, event | category | flops | bytes accessed | tf_op | source)
XLA Modules:
  0.0 303.4 jit_solution(6321874885541037050)
XLA Ops:
  6.5 0.0 all-gather.4.cloned.1.call-start
  6.5 0.7 all-gather.4.cloned.1.call-update
  7.3 0.0 all-gather.6.cloned.1.call-start
  7.3 0.7 all-gather.6.cloned.1.call-update
  8.0 0.0 all-gather.8.cloned.1.call-start
  8.1 0.7 all-gather.8.cloned.1.call-update
  8.7 0.0 copy-start.1
  8.8 0.8 reduce_window_sum.11
  9.5 0.7 add_select_fusion
  10.2 0.7 select_reduce_fusion.4
  10.9 0.1 constant_dynamic-slice_fusion
  11.0 0.6 fusion.84
  16.7 1.4 reshape.518
  20.7 1.6 pad_dynamic-slice_fusion.3
  22.2 5.1 %collective-permute-start = (bf16[256,1024]{1,0:T(8,128)(2,1)S(1)}, bf16[256,1024]{1,0:T(8,128)(2,1)S(1)}, u32[]{:S(2)}, u32[]{:S(2)}) collective-permute-start(bf16[256,1024]{1,0:T(8,128)(2,1)S(1)} %get-tuple-element.44), channel_id=1, source_target_pairs={{0,128},{8,136},{16,144},{24,152},{32,160},{40,168},{48,176},{56,1... | collective-permute-start | bytes 1572872 | tf_op jit(solution)/shard_map/ppermute | solution.py:10
  27.3 5.7 %collective-permute-start.1 = (bf16[256,1024]{1,0:T(8,128)(2,1)S(1)}, bf16[256,1024]{1,0:T(8,128)(2,1)}, u32[]{:S(2)}, u32[]{:S(2)}) collective-permute-start(bf16[256,1024]{1,0:T(8,128)(2,1)S(1)} %get-tuple-element.45), channel_id=1, source_target_pairs={{0,256},{8,264},{16,272},{24,280},{32,288},{40,296},{48,304},{56,3... | collective-permute-start | bytes 1572872 | tf_op jit(solution)/shard_map/ppermute | solution.py:10
  33.0 5.0 %collective-permute-start.2 = (bf16[256,1024]{1,0:T(8,128)(2,1)S(1)}, bf16[256,1024]{1,0:T(8,128)(2,1)}, u32[]{:S(2)}, u32[]{:S(2)}) collective-permute-start(bf16[256,1024]{1,0:T(8,128)(2,1)S(1)} %get-tuple-element.46), channel_id=1, source_target_pairs={{0,384},{8,392},{16,400},{24,408},{32,416},{40,424},{48,432},{56,4... | collective-permute-start | bytes 1572872 | tf_op jit(solution)/shard_map/ppermute | solution.py:10
  38.0 0.6 gather_fusion
  38.6 0.2 select_reduce_fusion.5
  38.8 0.1 select_reduce_fusion.2
  39.0 0.0 copy-done.1
  39.0 0.8 slice_reduce_fusion.29
  39.8 0.3 slice_reduce_fusion.30
  40.1 0.1 compare_and_fusion.31
  40.2 1.1 collective-permute-done
  41.2 0.0 copy-start
  41.2 27.6 %collective-permute-done.1 = bf16[256,1024]{1,0:T(8,128)(2,1)} collective-permute-done((bf16[256,1024]{1,0:T(8,128)(2,1)S(1)}, bf16[256,1024]{1,0:T(8,128)(2,1)}, u32[]{:S(2)}, u32[]{:S(2)}) %collective-permute-start.1) | collective-permute-done | bytes 524320 | tf_op jit(solution)/shard_map/ppermute | solution.py:10
  68.8 11.9 %collective-permute-done.2 = bf16[256,1024]{1,0:T(8,128)(2,1)} collective-permute-done((bf16[256,1024]{1,0:T(8,128)(2,1)S(1)}, bf16[256,1024]{1,0:T(8,128)(2,1)}, u32[]{:S(2)}, u32[]{:S(2)}) %collective-permute-start.2) | collective-permute-done | bytes 524320 | tf_op jit(solution)/shard_map/ppermute | solution.py:10
  80.7 0.0 copy-done
  80.7 1.5 pad_maximum_fusion
  82.3 2.2 gather_fusion.1
  84.5 0.2 broadcast_select_fusion
  84.7 31.2 %all-gather.4.cloned.1.call-done = bf16[1536,512]{1,0:T(8,128)(2,1)} async-done(((bf16[24,512]{1,0:T(8,128)(2,1)}), bf16[1536,512]{1,0:T(8,128)(2,1)}) %all-gather.4.cloned.1.call-update) | async-done | bytes 1572880 | tf_op jit(solution)/shard_map/all_gather | solution.py:91
  116.0 1.5 fusion.62
  117.5 2.5 convolution_add_fusion.1
  120.0 0.0 copy-start.10
  120.0 78.9 %all-gather.6.cloned.1.call-done = bf16[512,1536]{1,0:T(8,128)(2,1)} async-done(((bf16[8,1536]{1,0:T(8,128)(2,1)}), bf16[512,1536]{1,0:T(8,128)(2,1)}) %all-gather.6.cloned.1.call-update) | async-done | bytes 1572880 | tf_op jit(solution)/shard_map/all_gather | solution.py:92
  198.9 3.2 %convert_reduce_fusion = (f32[512]{0:T(512)S(1)}, bf16[512,1536]{1,0:T(8,128)(2,1)S(1)}) fusion(bf16[512,1536]{1,0:T(8,128)(2,1)} %all-gather.6.cloned.1.call-done, f32[512,512]{1,0:T(8,128)} %convolution_add_fusion.1, bf16[1536,512]{1,0:T(8,128)(2,1)} %all-gather.4.cloned.1.call-done, bf16[512,1024]{1,0:T(8,128)(2,1)S(1)} %broadcast_select_fusion), kind=kOutput, calls=%fused_computation.7 | convolution fusion | flops 1076887040 | bytes 5244928 | tf_op jit(solution)/shard_map/dot_general | solution.py:116
  202.1 0.6 fusion.8
  202.7 59.3 %all-gather.8.cloned.1.call-done = bf16[2,1536,1536]{1,2,0:T(8,128)(2,1)} async-done(((bf16[2,1536,192]{1,2,0:T(8,128)(2,1)}), bf16[2,1536,1536]{1,2,0:T(8,128)(2,1)}) %all-gather.8.cloned.1.call-update) | async-done | bytes 9437200 | tf_op jit(solution)/shard_map/all_gather | solution.py:118
  261.9 0.0 copy-done.10
  261.9 0.0 copy-start.9
  261.9 5.2 %fusion.7 = f32[512,1536]{1,0:T(8,128)S(1)} fusion(bf16[2,1536,1536]{1,2,0:T(8,128)(2,1)} %all-gather.8.cloned.1.call-done, bf16[512,1536]{1,0:T(8,128)(2,1)S(1)} %get-tuple-element.85, f32[1536]{0:T(1024)S(1)} %copy-done.10, f32[512]{0:T(512)S(1)} %add_rsqrt_fusion.1, f32[512]{0:T(512)S(1)} %broadcast_multiply_fusion.1), kind=kOutput, calls=%fused_computation.13 | convolution fusion | flops 2421424128 | bytes 9447424 | tf_op jit(solution)/shard_map/dot_general | solution.py:51
  267.1 0.0 copy-done.9
  267.1 0.0 copy-start.2
  267.1 0.0 copy-start.3
  267.1 0.0 copy-start.4
  267.2 0.0 copy-start.5
  267.2 0.0 copy-start.6
  267.2 0.0 copy-start.7
  267.2 2.7 fusion.53
  269.9 0.0 copy-done.2
  269.9 0.0 copy-done.3
  269.9 0.0 copy-done.4
  269.9 0.0 copy-done.5
  269.9 0.0 copy-done.6
  269.9 0.0 copy-done.7
  269.9 24.0 %fusion.83 = (f32[512]{0:T(512)S(1)}, f32[512,1536]{1,0:T(8,128)S(1)}) fusion(f32[1536]{0:T(1024)S(1)} %copy-done.6, pred[512]{0:T(512)(128)(4,1)S(1)} %get-tuple-element.48, f32[1536]{0:T(1024)S(1)} %copy-done.7, pred[512]{0:T(512)(128)(4,1)S(1)} %get-tuple-element.49, f32[1536]{0:T(1024)S(1)} %get-tuple-element.6, ...), kind=kLoop, calls=%fused_computation.211 | loop fusion | flops 73137664 | bytes 6499840 | tf_op jit(solution)/shard_map/reduce_sum | solution.py:30
  293.9 0.0 copy-start.8
  294.0 0.4 multiply_reduce_fusion
  294.4 0.2 copy-done.8
  294.6 2.2 multiply_convert_fusion
  (11 shorter events, 0.1 us)
Async XLA Ops:
  6.5 109.4 %all-gather.4.cloned.1.call-start = ((), (), s32[]{:S(2)}) async-start(), calls=%async_computation | async-start | bytes 1597440 | tf_op jit(solution)/shard_map/all_gather | solution.py:91
  7.3 191.6 %all-gather.6.cloned.1.call-start = ((), (), s32[]{:S(2)}) async-start(), calls=%async_computation.1 | async-start | bytes 1597440 | tf_op jit(solution)/shard_map/all_gather | solution.py:92
  8.0 253.9 %all-gather.8.cloned.1.call-start = ((), (), s32[]{:S(2)}) async-start(), calls=%async_computation.2 | async-start | bytes 10616832 | tf_op jit(solution)/shard_map/all_gather | solution.py:118
  8.7 30.2 %copy-start.1 = (f32[31,1536]{1,0:T(8,128)S(1)}, f32[31,1536]{1,0:T(8,128)}, u32[]{:S(2)}) copy-start(f32[31,1536]{1,0:T(8,128)} %param.15) | copy-start | bytes 571396
  22.2 19.0 %collective-permute-start = (bf16[256,1024]{1,0:T(8,128)(2,1)S(1)}, bf16[256,1024]{1,0:T(8,128)(2,1)S(1)}, u32[]{:S(2)}, u32[]{:S(2)}) collective-permute-start(bf16[256,1024]{1,0:T(8,128)(2,1)S(1)} %get-tuple-element.44), channel_id=1, source_target_pairs={{0,128},{8,136},{16,144},{24,152},{32,160},{40,168},{48,176},{56,1... | collective-permute-start | bytes 1572872 | tf_op jit(solution)/shard_map/ppermute | solution.py:10
  27.3 41.5 %collective-permute-start.1 = (bf16[256,1024]{1,0:T(8,128)(2,1)S(1)}, bf16[256,1024]{1,0:T(8,128)(2,1)}, u32[]{:S(2)}, u32[]{:S(2)}) collective-permute-start(bf16[256,1024]{1,0:T(8,128)(2,1)S(1)} %get-tuple-element.45), channel_id=1, source_target_pairs={{0,256},{8,264},{16,272},{24,280},{32,288},{40,296},{48,304},{56,3... | collective-permute-start | bytes 1572872 | tf_op jit(solution)/shard_map/ppermute | solution.py:10
  33.0 47.8 %collective-permute-start.2 = (bf16[256,1024]{1,0:T(8,128)(2,1)S(1)}, bf16[256,1024]{1,0:T(8,128)(2,1)}, u32[]{:S(2)}, u32[]{:S(2)}) collective-permute-start(bf16[256,1024]{1,0:T(8,128)(2,1)S(1)} %get-tuple-element.46), channel_id=1, source_target_pairs={{0,384},{8,392},{16,400},{24,408},{32,416},{40,424},{48,432},{56,4... | collective-permute-start | bytes 1572872 | tf_op jit(solution)/shard_map/ppermute | solution.py:10
  41.2 39.5 %copy-start = (bf16[256,1024]{1,0:T(8,128)(2,1)}, bf16[256,1024]{1,0:T(8,128)(2,1)S(1)}, u32[]{:S(2)}) copy-start(bf16[256,1024]{1,0:T(8,128)(2,1)S(1)} %collective-permute-done) | copy-start | bytes 1572868
  120.0 142.0 %copy-start.10 = (f32[1536]{0:T(1024)S(1)}, f32[1536]{0:T(1024)}, u32[]{:S(2)}) copy-start(f32[1536]{0:T(1024)} %param.16) | copy-start | bytes 18436
  261.9 5.2 %copy-start.9 = (bf16[2,1536,1536]{1,2,0:T(8,128)(2,1)S(1)}, bf16[2,1536,1536]{1,2,0:T(8,128)(2,1)}, u32[]{:S(2)}) copy-start(bf16[2,1536,1536]{1,2,0:T(8,128)(2,1)} %all-gather.8.cloned.1.call-done) | copy-start | bytes 28311556
  267.1 2.8 copy-start.2
  267.1 2.8 copy-start.3
  267.1 2.8 copy-start.4
  267.2 2.8 copy-start.5
  267.2 2.8 copy-start.6
  267.2 2.8 copy-start.7
  293.9 0.7 copy-start.8
Sparse Core Ops, SparseCore 0:
  10.4 105.5 all-gather.3
  119.0 79.7 all-gather.5
  201.0 60.9 all-gather.7
where the time goes:
time: 304 us; the launch traced here: 303 us
  waiting for transfers between devices  212 us (70%)
  other arithmetic  31.5 us (10%)
  between operations  21 us (7%)
  starting transfers between devices  15.8 us (5%)
  matrix products  15 us (5%)
  local copies, waits for them, and re-layouts  7.95 us (3%)
    all_gather x1, waiting for transfers between devices, body(): lax.all_gather(proj_weight, 'dp', axis=0, tiled=True)  78.9 us
    all_gather x1, waiting for transfers between devices, body(): weight_part = lax.all_gather(point_weight, 'fsdp', axis=2, tiled=True)  59.3 us
    ppermute x3, waiting for transfers between devices, passed_along(): return lax.ppermute(value, axis, pairs)  40.6 us
    all_gather x1, waiting for transfers between devices, body(): lax.all_gather(conv_weight, 'dp', axis=0, tiled=True)  31.2 us
    reduce_sum x1, other arithmetic, layer_norm(): centered = values - jnp.mean(values, axis=-1, keepdims=True)  24 us
    ppermute x3, starting transfers between devices, passed_along(): return lax.ppermute(value, axis, pairs)  15.7 us
  transfers between devices with their start and end apart: 6, of which 6 were waited for; matrix products, arithmetic and copies ran while one was open for 7% of the time, Pallas kernels for 0%

commit v1 on v0

--- a/solution.py
+++ b/solution.py
@@ -2,6 +2,13 @@
 import jax.numpy as jnp
 from jax import lax
 from jax.sharding import PartitionSpec as P
+
+
+def heads_define(buf, in_dim):
+    size_here = lax.axis_size("fsdp")
+    made = [size_here if q == in_dim else 1 for q in range(buf.ndim)]
+    block_next = jnp.tile(buf, made)
+    return lax.all_to_all(block_next, "fsdp", split_axis=in_dim, concat_axis=in_dim, tiled=True)
 
 
 def passed_along(value, axis, steps):
@@ -115,7 +122,7 @@
     front = frontend(packed, positions == 0, conv_full)
     projected = jnp.dot(front, proj_full, preferred_element_type=jnp.float32).astype(jnp.bfloat16)
     normed = layer_norm(projected.astype(jnp.float32), gain_first).astype(jnp.bfloat16)
-    weight_part = lax.all_gather(point_weight, "fsdp", axis=2, tiled=True)
+    weight_part = heads_define(point_weight, 2)
     gated = gate_product(normed, weight_part[0], weight_part[1])
     mixed = depthwise(gated, depth_weight, positions, lengths)
     scaled = layer_norm(mixed, gain_second)

time: 304 us -> 377 us (1.24); the launches traced: 303 us -> 372 us
  local copies, waits for them, and re-layouts: 7.95 us -> 126 us
  waiting for transfers between devices: 212 us -> 159 us
  starting transfers between devices: 15.8 us -> 20.4 us
    all_gather x1 -> x0, waiting for transfers between devices: 59.3 us -> none  [body(): weight_part = lax.all_gather(point_weight, 'fsdp', axis=2, tiled=True)]
    another operation x0 -> x2, local copies, waits for them, and re-layouts: none -> 54.3 us  [heads_define(): block_next = jnp.tile(buf, made)]
    unnamed x22 -> x32, local copies, waits for them, and re-layouts: 0.26 us -> 45.1 us
    slice x0 -> x1, local copies, waits for them, and re-layouts: none -> 19.6 us  [body(): gated = gate_product(normed, weight_part[0], weight_part[1])]
    all_gather x1, waiting for transfers between devices: 31.2 us -> 45 us  [body(): lax.all_gather(conv_weight, 'dp', axis=0, tiled=True)]
    all_to_all x0 -> x1, starting transfers between devices: none -> 11.9 us  [heads_define(): lax.all_to_all(block_next, 'fsdp', split_axis=in_dim, concat_axis=in_dim,...]
    ppermute x3, starting transfers between devices: 15.7 us -> 8.43 us  [passed_along(): return lax.ppermute(value, axis, pairs)]
    ppermute x3, waiting for transfers between devices: 40.6 us -> 34.7 us  [passed_along(): return lax.ppermute(value, axis, pairs)]
  transfers between devices with their start and end apart: 6 -> 6, of which waited for: 6 -> 4; matrix products, arithmetic and copies ran while one was open for 7% -> 5% of each run, Pallas kernels for 0% -> 0%
where the time goes in v1:
time: 377 us; the launch traced here: 372 us
  waiting for transfers between devices  159 us (42%)
  local copies, waits for them, and re-layouts  126 us (33%)
  other arithmetic  30 us (8%)
  between operations  21.1 us (6%)
  starting transfers between devices  20.4 us (5%)
  matrix products  15 us (4%)
    all_gather x1, waiting for transfers between devices, body(): lax.all_gather(proj_weight, 'dp', axis=0, tiled=True)  78.4 us
    another operation x2, local copies, waits for them, and re-layouts, heads_define(): block_next = jnp.tile(buf, made)  54.3 us
    unnamed x32, local copies, waits for them, and re-layouts  45.1 us
    all_gather x1, waiting for transfers between devices, body(): lax.all_gather(conv_weight, 'dp', axis=0, tiled=True)  45 us
    ppermute x3, waiting for transfers between devices, passed_along(): return lax.ppermute(value, axis, pairs)  34.7 us
    reduce_sum x1, other arithmetic, layer_norm(): centered = values - jnp.mean(values, axis=-1, keepdims=True)  23.9 us
    slice x1, local copies, waits for them, and re-layouts, body(): gated = gate_product(normed, weight_part[0], weight_part[1])  19.6 us
    all_to_all x1, starting transfers between devices, heads_define(): lax.all_to_all(block_next, 'fsdp', split_axis=in_dim, concat_axis=in_dim,...  11.9 us
  transfers between devices with their start and end apart: 6, of which 4 were waited for; matrix products, arithmetic and copies ran while one was open for 5% of the time, Pallas kernels for 0%

profile of v1, /device:TPU:1, one launch (start us, length us, event | category | flops | bytes accessed | tf_op | source)
XLA Modules:
  0.0 372.2 jit_solution(3981288067965822712)
XLA Ops:
  6.5 2.2 tile.4
  8.7 52.2 %copy.31 = bf16[2,1536,1536]{1,0,2:T(2,128)(2,1)} copy(bf16[2,1536,1536]{1,2,0:T(8,128)(2,1)S(1)} %bitcast.41) | data formatting | bytes 18874368 | tf_op jit(solution)/shard_map/tile | solution.py:10
  60.9 11.9 %all-to-all-start = ((bf16[2,1536,1536]{1,0,2:T(2,128)(2,1)}), bf16[2,1536,1536]{1,0,2:T(2,128)(2,1)}, u32[]{:S(2)}, u32[]{:S(2)}) async-start(bf16[2,1536,1536]{1,0,2:T(2,128)(2,1)} %copy.31), calls=%async_computation | async-start | bytes 18874368 | tf_op jit(solution)/shard_map/all_to_all | solution.py:11
  72.8 0.0 all-gather.3.cloned.1.call-start
  72.8 0.7 all-gather.3.cloned.1.call-update
  73.5 0.0 all-gather.5.cloned.1.call-start
  73.6 0.7 all-gather.5.cloned.1.call-update
  74.3 0.0 copy-done.10
  74.3 0.0 copy-done.13
  74.4 0.1 constant_dynamic-slice_fusion
  74.5 0.6 fusion.102
  80.0 0.0 copy-done.1
  80.0 0.4 reshape.522
  82.9 2.4 pad_dynamic-slice_fusion.3
  85.3 1.9 collective-permute-start.2
  87.2 2.1 collective-permute-start.1
  89.3 4.4 %collective-permute-start = (bf16[256,1024]{1,0:T(8,128)(2,1)S(1)}, bf16[256,1024]{1,0:T(8,128)(2,1)}, u32[]{:S(2)}, u32[]{:S(2)}) collective-permute-start(bf16[256,1024]{1,0:T(8,128)(2,1)S(1)} %get-tuple-element.46), channel_id=1, source_target_pairs={{0,128},{8,136},{16,144},{24,152},{32,160},{40,168},{48,176},{56,1... | collective-permute-start | bytes 1572872 | tf_op jit(solution)/shard_map/ppermute | solution.py:17
  93.7 0.6 gather_fusion
  94.4 0.2 select_reduce_fusion.5
  94.6 0.1 select_reduce_fusion.2
  94.7 0.6 pad_clamp_fusion
  95.3 0.0 copy-done.4
  95.3 0.8 slice_reduce_fusion.29
  96.1 0.3 slice_reduce_fusion.30
  96.4 0.0 copy-start.11
  96.4 0.1 compare_and_fusion.31
  96.5 31.2 %collective-permute-done.2 = bf16[256,1024]{1,0:T(8,128)(2,1)S(1)} collective-permute-done((bf16[256,1024]{1,0:T(8,128)(2,1)}, bf16[256,1024]{1,0:T(8,128)(2,1)S(1)}, u32[]{:S(2)}, u32[]{:S(2)}) %collective-permute-start.2) | collective-permute-done | bytes 524320 | tf_op jit(solution)/shard_map/ppermute | solution.py:17
  127.7 0.0 collective-permute-done.1
  127.7 3.5 collective-permute-done
  131.2 0.0 copy-done.2
  131.2 0.0 copy-done.3
  131.2 1.5 pad_maximum_fusion
  132.7 0.0 copy-done.11
  132.8 2.1 gather_fusion.1
  134.8 0.2 broadcast_select_fusion
  135.0 45.0 %all-gather.3.cloned.1.call-done = bf16[1536,512]{1,0:T(8,128)(2,1)} async-done(((bf16[24,512]{1,0:T(8,128)(2,1)}), bf16[1536,512]{1,0:T(8,128)(2,1)}) %all-gather.3.cloned.1.call-update) | async-done | bytes 1572880 | tf_op jit(solution)/shard_map/all_gather | solution.py:98
  180.0 1.5 fusion.79
  181.5 2.5 convolution_add_fusion.1
  184.0 78.4 %all-gather.5.cloned.1.call-done = bf16[512,1536]{1,0:T(8,128)(2,1)} async-done(((bf16[8,1536]{1,0:T(8,128)(2,1)}), bf16[512,1536]{1,0:T(8,128)(2,1)}) %all-gather.5.cloned.1.call-update) | async-done | bytes 1572880 | tf_op jit(solution)/shard_map/all_gather | solution.py:99
  262.4 3.2 convert_reduce_fusion
  265.6 0.6 fusion.21
  266.2 0.0 all-to-all-done
  266.2 19.6 %fusion.101 = (bf16[1,1536,1536]{1,0,2:T(2,128)(2,1)}, bf16[1,1536,1536]{1,0,2:T(2,128)(2,1)}) fusion(bf16[2,1536,1536]{1,0,2:T(2,128)(2,1)} %all-to-all-done), kind=kLoop, calls=%fused_computation.213 | loop fusion | bytes 18874368 | tf_op jit(solution)/shard_map/slice | solution.py:126
  285.7 22.4 %copy.35 = bf16[1,1536,1536]{2,1,0:T(8,128)(2,1)} copy(bf16[1,1536,1536]{1,0,2:T(2,128)(2,1)} %get-tuple-element.44) | data formatting | bytes 9437184
  308.1 22.4 %copy.34 = bf16[1,1536,1536]{2,1,0:T(8,128)(2,1)} copy(bf16[1,1536,1536]{1,0,2:T(2,128)(2,1)} %get-tuple-element.43) | data formatting | bytes 9437184
  330.6 0.0 copy-done.14
  330.6 5.1 %fusion.18 = f32[512,1536]{1,0:T(8,128)S(1)} fusion(bf16[1,1536,1536]{2,1,0:T(8,128)(2,1)} %copy.35, bf16[512,1536]{1,0:T(8,128)(2,1)S(1)} %get-tuple-element.87, f32[1536]{0:T(1024)S(1)} %copy-done.14, f32[512]{0:T(512)S(1)} %add_rsqrt_fusion.1, f32[512]{0:T(512)S(1)} %broadcast_multiply_fusion.1), kind=kOutput, calls=%fused_computation.14 | convolution fusion | flops 2422210560 | bytes 9447424 | tf_op jit(solution)/shard_map/dot_general | solution.py:58
  335.7 0.0 copy-done
  335.7 0.0 copy-start.5
  335.7 0.0 copy-start.6
  335.7 0.0 copy-start.7
  335.7 0.0 copy-start.8
  335.8 0.0 copy-start.9
  335.8 2.7 fusion.68
  338.4 0.0 copy-done.5
  338.4 0.0 copy-done.6
  338.5 0.0 copy-done.7
  338.5 0.0 copy-done.8
  338.5 0.0 copy-done.9
  338.5 23.9 %fusion.100 = (f32[512]{0:T(512)S(1)}, f32[512,1536]{1,0:T(8,128)S(1)}) fusion(f32[1536]{0:T(1024)S(1)} %copy-done.8, pred[512]{0:T(512)(128)(4,1)S(1)} %get-tuple-element.50, f32[1536]{0:T(1024)S(1)} %copy-done.9, pred[512]{0:T(512)(128)(4,1)S(1)} %get-tuple-element.51, f32[1536]{0:T(1024)S(1)} %get-tuple-element.6, ...), kind=kLoop, calls=%fused_computation.212 | loop fusion | flops 73137664 | bytes 6499840 | tf_op jit(solution)/shard_map/reduce_sum | solution.py:37
  362.4 0.0 copy-start.12
  362.4 0.4 multiply_reduce_fusion
  362.9 0.2 copy-done.12
  363.1 2.2 multiply_convert_fusion
  (21 shorter events, 0.2 us)
Async XLA Ops:
  60.9 13.4 %copy-start.10 = (s32[1,64,4]{1,2,0:T(4,128)S(1)}, s32[1,64,4]{1,2,0:T(4,128)}, u32[]{:S(2)}) copy-start(s32[1,64,4]{1,2,0:T(4,128)} %param.10) | copy-start | bytes 3076
  60.9 13.5 %copy-start.13 = (s32[1,64,4]{1,2,0:T(4,128)S(1)}, s32[1,64,4]{1,2,0:T(4,128)}, u32[]{:S(2)}) copy-start(s32[1,64,4]{1,2,0:T(4,128)} %param.11) | copy-start | bytes 3076
  60.9 19.1 %copy-start.1 = (bf16[1024,512]{1,0:T(8,128)(2,1)S(1)}, bf16[1024,512]{1,0:T(8,128)(2,1)}, u32[]{:S(2)}) copy-start(bf16[1024,512]{1,0:T(8,128)(2,1)} %param.9) | copy-start | bytes 3145732
  60.9 205.3 %all-to-all-start = ((bf16[2,1536,1536]{1,0,2:T(2,128)(2,1)}), bf16[2,1536,1536]{1,0,2:T(2,128)(2,1)}, u32[]{:S(2)}, u32[]{:S(2)}) async-start(bf16[2,1536,1536]{1,0,2:T(2,128)(2,1)} %copy.31), calls=%async_computation | async-start | bytes 18874368 | tf_op jit(solution)/shard_map/all_to_all | solution.py:11
  72.8 22.5 %copy-start.4 = (f32[31,1536]{1,0:T(8,128)S(1)}, f32[31,1536]{1,0:T(8,128)}, u32[]{:S(2)}) copy-start(f32[31,1536]{1,0:T(8,128)} %param.15) | copy-start | bytes 571396
  72.8 107.2 %all-gather.3.cloned.1.call-start = ((), (), s32[]{:S(2)}) async-start(), calls=%async_computation.1 | async-start | bytes 1597440 | tf_op jit(solution)/shard_map/all_gather | solution.py:98
  73.5 188.8 %all-gather.5.cloned.1.call-start = ((), (), s32[]{:S(2)}) async-start(), calls=%async_computation.2 | async-start | bytes 1597440 | tf_op jit(solution)/shard_map/all_gather | solution.py:99
  85.3 42.4 %collective-permute-start.2 = (bf16[256,1024]{1,0:T(8,128)(2,1)}, bf16[256,1024]{1,0:T(8,128)(2,1)S(1)}, u32[]{:S(2)}, u32[]{:S(2)}) collective-permute-start(bf16[256,1024]{1,0:T(8,128)(2,1)} %get-tuple-element.48), channel_id=1, source_target_pairs={{0,384},{8,392},{16,400},{24,408},{32,416},{40,424},{48,432},{56,4... | collective-permute-start | bytes 1572872 | tf_op jit(solution)/shard_map/ppermute | solution.py:17
  87.2 40.5 %collective-permute-start.1 = (bf16[256,1024]{1,0:T(8,128)(2,1)S(1)}, bf16[256,1024]{1,0:T(8,128)(2,1)S(1)}, u32[]{:S(2)}, u32[]{:S(2)}) collective-permute-start(bf16[256,1024]{1,0:T(8,128)(2,1)S(1)} %get-tuple-element.47), channel_id=1, source_target_pairs={{0,256},{8,264},{16,272},{24,280},{32,288},{40,296},{48,304},{56,3... | collective-permute-start | bytes 1572872 | tf_op jit(solution)/shard_map/ppermute | solution.py:17
  89.3 41.9 %collective-permute-start = (bf16[256,1024]{1,0:T(8,128)(2,1)S(1)}, bf16[256,1024]{1,0:T(8,128)(2,1)}, u32[]{:S(2)}, u32[]{:S(2)}) collective-permute-start(bf16[256,1024]{1,0:T(8,128)(2,1)S(1)} %get-tuple-element.46), channel_id=1, source_target_pairs={{0,128},{8,136},{16,144},{24,152},{32,160},{40,168},{48,176},{56,1... | collective-permute-start | bytes 1572872 | tf_op jit(solution)/shard_map/ppermute | solution.py:17
  96.4 36.3 %copy-start.11 = (s32[1024]{0:T(1024)S(1)}, s32[1024]{0:T(1024)}, u32[]{:S(2)}) copy-start(s32[1024]{0:T(1024)} %pad_clamp_fusion) | copy-start | bytes 12292
  127.7 3.5 copy-start.2
  127.7 3.5 copy-start.3
  308.1 22.4 %copy-start.14 = (f32[1536]{0:T(1024)S(1)}, f32[1536]{0:T(1024)}, u32[]{:S(2)}) copy-start(f32[1536]{0:T(1024)} %param.16) | copy-start | bytes 18436
  330.6 5.1 %copy-start = (bf16[1,1536,1536]{2,1,0:T(8,128)(2,1)S(1)}, bf16[1,1536,1536]{2,1,0:T(8,128)(2,1)}, u32[]{:S(2)}) copy-start(bf16[1,1536,1536]{2,1,0:T(8,128)(2,1)} %copy.34) | copy-start | bytes 14155780
  335.7 2.7 copy-start.5
  335.7 2.7 copy-start.6
  335.7 2.7 copy-start.7
  335.7 2.7 copy-start.8
  335.8 2.7 copy-start.9
  362.4 0.7 copy-start.12
Sparse Core Ops, SparseCore 0:
  76.7 103.2 all-gather.2
  183.1 79.2 all-gather.4
